TPU v7x, 256 devices: a whole 4x4x8 slice. The times are simulated.
256 devices in a mesh: leaf: 64 (over y, x, z_hi, core), blk: 4 (over z_lo).
Axes of the slice: x: 4, y: 4, z: 8 (z_hi: 2, z_lo: 4; z = z_hi * 4 + z_lo), core: 2. Of those that a mesh axis runs over, the one named last changes fastest.
Arguments:
- interface: bfloat16 [262144, 512], P(('leaf', 'blk')), may hold values from -6 to 6
- owners: int32 [262144, 1], P(('leaf', 'blk')), may hold values from 0 to 63; in each aligned block of 1024 rows (0 to 1023, 1024 to 2047, ...) at most 32 rows name the same one
- keep_proj: bfloat16 [3, 512, 512], replicated, may hold values from -0.25 to 0.25
- sibling_proj: bfloat16 [3, 512, 512], replicated, may hold values from -0.25 to 0.25
- coupling: bfloat16 [64, 512, 512], P('leaf'), may hold values from -0.25 to 0.25
- pattern: int32 [64, 8, 8], P('leaf'), may hold values 0 or 1
Outputs:
- coupled: bfloat16 [262144, 512], P(('leaf', 'blk'))
Inputs may be any that keep to these rules, and one draw needn't show every extreme that they name: `owners`: among the 1024 rows of one device no owner is named by more than 32 rows, a bound that some block reaches.
All inputs are finite; a program needn't handle non-finite values. No bound on the sum of `pattern` on one device may be relied on, other than what follows from the above.
Results may differ from a plain program's by a relative error of at most 0.0075.
Values may be sent and summed in bfloat16 or wider, within the bound.
A program may use at most 64 MiB of HBM per device.

v0:
```python
import jax
import jax.numpy as jnp
from jax import lax
from jax.sharding import PartitionSpec as P

BS = 64
LEVELS = 3


epsilon = 1e-06


def swapped(value, axis, bit):
    mask = 2**bit
    pairs = [(source, source ^ mask) for source in range(lax.axis_size(axis))]
    return lax.ppermute(value, axis, pairs)


def local(interface, owners, keep_proj, sibling_proj, coupling, pattern):
    row_count, features = interface.shape
    current = interface
    for tree_level in range(LEVELS):
        sibling = swapped(current, "leaf", tree_level)
        combined = jnp.dot(current, keep_proj[tree_level], preferred_element_type=jnp.float32)
        combined = combined + jnp.dot(
            sibling, sibling_proj[tree_level], preferred_element_type=jnp.float32
        )
        scale_rows = lax.rsqrt(jnp.mean(combined * combined, axis=1, keepdims=True) + epsilon)
        current = (combined * scale_rows).astype(jnp.bfloat16)
    leaves = lax.axis_size("leaf")
    capacity = 2 * row_count // leaves
    target = owners[:, 0]
    onehot = (target[:, None] == jnp.arange(leaves, dtype=jnp.int32)[None, :]).astype(jnp.int32)
    slot_index = jnp.sum(jnp.cumsum(onehot, axis=0) * onehot, axis=1) - 1
    position = target * capacity + slot_index
    outgoing = jnp.zeros((leaves * capacity, features), jnp.bfloat16).at[position].set(current)
    expanded = jnp.repeat(jnp.repeat(pattern[0], BS, axis=0), BS, axis=1)
    masked = coupling[0] * expanded.astype(jnp.bfloat16)
    sectioned = outgoing.reshape(leaves, capacity, features)
    product = jnp.einsum(
        "...m,mn->...n",
        lax.all_to_all(sectioned, "leaf", split_axis=0, concat_axis=0, tiled=True),
        masked,
        preferred_element_type=jnp.float32,
    )
    result = product.astype(jnp.bfloat16)
    returned = lax.all_to_all(result, "leaf", split_axis=0, concat_axis=0, tiled=True)
    returned = returned.reshape(leaves * capacity, features)
    return returned[position]


def solution(mesh):
    in_specs = (
        P(("leaf", "blk"), None),
        P(("leaf", "blk"), None),
        P(),
        P(),
        P("leaf", None, None),
        P("leaf", None, None),
    )
    out_specs = P(("leaf", "blk"), None)
    return jax.shard_map(local, mesh=mesh, in_specs=in_specs, out_specs=out_specs, check_vma=False)
```

profile of v0, /device:TPU:33, one launch (start us, length us, event | category | flops | bytes accessed | tf_op | source)
XLA Modules:
  0.0 220.0 jit_solution(785856043478025775)
XLA Ops:
  0.0 0.7 collective-permute-start
  0.7 2.1 fusion.10
  2.8 0.4 collective-permute-done
  3.2 1.8 multiply_reduce_fusion.2
  5.0 0.0 copy-start.3
  5.0 0.0 copy-start
  5.0 0.3 multiply_convert_fusion.2
  5.3 6.1 %collective-permute-start.1 = (bf16[1024,512]{0,1:T(8,128)(2,1)S(1)}, bf16[1024,512]{0,1:T(8,128)(2,1)}, u32[]{:S(2)}, u32[]{:S(2)}) collective-permute-start(bf16[1024,512]{0,1:T(8,128)(2,1)S(1)} %multiply_convert_fusion.2), channel_id=1, source_target_pairs={{0,8},{4,12},{8,0},{12,4},{16,24},{20,28},{24,16},{28,20},{32,40},... | collective-permute-start | bytes 3145736 | tf_op jit(solution)/shard_map/ppermute | solution.py:16
  11.4 0.0 copy-done.3
  11.4 18.0 %reduce-window.6 = s32[64,8,128]{2,1,0:T(8,128)S(1)} reduce-window(s32[64,8,128]{2,1,0:T(8,128)S(1)} %fusion.20, s32[]{:T(128)} %constant.7.clone.1), window={size=1x1x128 pad=0_0x0_0x127_0}, to_apply=%region_0.0 | reduce-window | flops 8323072 | bytes 524292 | tf_op jit(solution)/shard_map/reduce-window
  29.4 0.1 slice.34
  29.6 0.1 copy.7
  29.8 0.1 copy.8
  29.9 0.0 copy-done
  29.9 0.0 copy-start.1
  29.9 0.8 fusion.7
  30.6 26.7 %collective-permute-done.1 = bf16[1024,512]{0,1:T(8,128)(2,1)} collective-permute-done((bf16[1024,512]{0,1:T(8,128)(2,1)S(1)}, bf16[1024,512]{0,1:T(8,128)(2,1)}, u32[]{:S(2)}, u32[]{:S(2)}) %collective-permute-start.1) | collective-permute-done | bytes 1048608 | tf_op jit(solution)/shard_map/ppermute | solution.py:16
  57.3 0.0 copy-done.1
  57.3 2.0 multiply_reduce_fusion.1
  59.3 0.3 multiply_convert_fusion.1
  59.6 1.3 collective-permute-start.2
  60.9 0.1 broadcast_add_fusion
  61.0 0.1 fusion.19
  61.1 0.8 fusion.4
  61.9 21.4 %collective-permute-done.2 = bf16[1024,512]{0,1:T(8,128)(2,1)S(1)} collective-permute-done((bf16[1024,512]{0,1:T(8,128)(2,1)S(1)}, bf16[1024,512]{0,1:T(8,128)(2,1)S(1)}, u32[]{:S(2)}, u32[]{:S(2)}) %collective-permute-start.2) | collective-permute-done | bytes 1048608 | tf_op jit(solution)/shard_map/ppermute | solution.py:16
  83.3 0.8 multiply_reduce_fusion
  84.1 0.3 multiply_convert_fusion
  84.4 0.5 copy.9
  84.9 6.7 %scatter_custom_fusion = bf16[2048,512]{1,0:T(8,128)(2,1)} fusion(s32[1024]{0:T(1024)S(1)} %bitcast.67, bf16[1024,512]{1,0:T(8,128)(2,1)S(1)} %copy.9, bf16[]{:T(256)} %constant.8.clone.1), kind=kCustom, calls=%fused_computation.12 | custom fusion | bytes 2097154 | tf_op jit(solution)/shard_map/scatter | solution.py:36
  91.6 0.0 copy-start.2
  91.6 0.0 copy-start.4
  91.6 14.3 %all-to-all-start = ((bf16[64,32,512]{2,1,0:T(8,128)(2,1)}), bf16[64,32,512]{2,1,0:T(8,128)(2,1)S(1)}, u32[]{:S(2)}, u32[]{:S(2)}) async-start(bf16[64,32,512]{2,1,0:T(8,128)(2,1)} %bitcast.12), calls=%async_computation | async-start | bytes 4194304 | tf_op jit(solution)/shard_map/all_to_all | solution.py:42
  105.9 0.0 copy-done.2
  105.9 0.2 copy.10
  106.1 0.0 copy-done.4
  106.2 0.1 copy.11
  106.2 0.1 broadcast_in_dim.7
  106.3 0.1 convert_element_type.37
  106.5 50.5 %all-to-all-done = bf16[64,32,512]{2,1,0:T(8,128)(2,1)S(1)} async-done(((bf16[64,32,512]{2,1,0:T(8,128)(2,1)}), bf16[64,32,512]{2,1,0:T(8,128)(2,1)S(1)}, u32[]{:S(2)}, u32[]{:S(2)}) %all-to-all-start) | async-done | bytes 2097184 | tf_op jit(solution)/shard_map/all_to_all | solution.py:42
  156.9 2.6 %convolution_convert_fusion = bf16[64,32,512]{2,1,0:T(8,128)(2,1)} fusion(bf16[64,32,512]{2,1,0:T(8,128)(2,1)S(1)} %all-to-all-done, bf16[512,512]{0,1:T(8,128)(2,1)S(1)} %bitcast_multiply_fusion), kind=kOutput, calls=%fused_computation.8 | convolution fusion | flops 1074790400 | bytes 4718592 | tf_op jit(solution)/shard_map/...m,mn->...n/dot_general | solution.py:40
  159.6 4.6 %all-to-all-start.1 = ((bf16[64,32,512]{2,1,0:T(8,128)(2,1)}), bf16[64,32,512]{2,1,0:T(8,128)(2,1)S(1)}, u32[]{:S(2)}, u32[]{:S(2)}) async-start(bf16[64,32,512]{2,1,0:T(8,128)(2,1)} %convolution_convert_fusion), calls=%async_computation.1 | async-start | bytes 4194304 | tf_op jit(solution)/shard_map/all_to_all | solution.py:47
  164.2 50.7 %all-to-all-done.1 = bf16[64,32,512]{2,1,0:T(8,128)(2,1)S(1)} async-done(((bf16[64,32,512]{2,1,0:T(8,128)(2,1)}), bf16[64,32,512]{2,1,0:T(8,128)(2,1)S(1)}, u32[]{:S(2)}, u32[]{:S(2)}) %all-to-all-start.1) | async-done | bytes 2097184 | tf_op jit(solution)/shard_map/all_to_all | solution.py:47
  214.9 5.1 %gather_fusion = bf16[1024,512]{1,0:T(8,128)(2,1)} fusion(bf16[2048,512]{1,0:T(8,128)(2,1)S(1)} %bitcast.62, s32[1024]{0:T(1024)S(1)} %broadcast_clamp_fusion), kind=kCustom, calls=%fused_computation | custom fusion | bytes 2101248 | tf_op jit(solution)/shard_map/gather | solution.py:49
  (11 shorter events, 0.1 us)
Async XLA Ops:
  0.0 3.2 %collective-permute-start = (bf16[1024,512]{1,0:T(8,128)(2,1)}, bf16[1024,512]{1,0:T(8,128)(2,1)S(1)}, u32[]{:S(2)}, u32[]{:S(2)}) collective-permute-start(bf16[1024,512]{1,0:T(8,128)(2,1)} %param.6), channel_id=1, source_target_pairs={{0,4},{4,0},{8,12},{12,8},{16,20},{20,16},{24,28},{28,24},{32,36},... | collective-permute-start | bytes 3145736 | tf_op jit(solution)/shard_map/ppermute | solution.py:16
  5.0 6.4 %copy-start.3 = (s32[1024,1]{0,1:T(1,128)S(1)}, s32[1024,1]{0,1:T(1,128)}, u32[]{:S(2)}) copy-start(s32[1024,1]{0,1:T(1,128)} %param.7) | copy-start | bytes 12292
  5.0 24.8 %copy-start = (bf16[3,512,512]{2,1,0:T(8,128)(2,1)S(1)}, bf16[3,512,512]{2,1,0:T(8,128)(2,1)}, u32[]{:S(2)}) copy-start(bf16[3,512,512]{2,1,0:T(8,128)(2,1)} %param.8) | copy-start | bytes 4718596
  5.3 52.0 %collective-permute-start.1 = (bf16[1024,512]{0,1:T(8,128)(2,1)S(1)}, bf16[1024,512]{0,1:T(8,128)(2,1)}, u32[]{:S(2)}, u32[]{:S(2)}) collective-permute-start(bf16[1024,512]{0,1:T(8,128)(2,1)S(1)} %multiply_convert_fusion.2), channel_id=1, source_target_pairs={{0,8},{4,12},{8,0},{12,4},{16,24},{20,28},{24,16},{28,20},{32,40},... | collective-permute-start | bytes 3145736 | tf_op jit(solution)/shard_map/ppermute | solution.py:16
  29.9 27.4 %copy-start.1 = (bf16[3,512,512]{2,1,0:T(8,128)(2,1)S(1)}, bf16[3,512,512]{2,1,0:T(8,128)(2,1)}, u32[]{:S(2)}) copy-start(bf16[3,512,512]{2,1,0:T(8,128)(2,1)} %param.9) | copy-start | bytes 4718596
  59.6 23.7 %collective-permute-start.2 = (bf16[1024,512]{0,1:T(8,128)(2,1)S(1)}, bf16[1024,512]{0,1:T(8,128)(2,1)S(1)}, u32[]{:S(2)}, u32[]{:S(2)}) collective-permute-start(bf16[1024,512]{0,1:T(8,128)(2,1)S(1)} %multiply_convert_fusion.1), channel_id=1, source_target_pairs={{0,16},{4,20},{8,24},{12,28},{16,0},{20,4},{24,8},{28,12},{32,48},... | collective-permute-start | bytes 3145736 | tf_op jit(solution)/shard_map/ppermute | solution.py:16
  91.6 14.3 %copy-start.2 = (bf16[1,512,512]{2,1,0:T(8,128)(2,1)S(1)}, bf16[1,512,512]{2,1,0:T(8,128)(2,1)}, u32[]{:S(2)}) copy-start(bf16[1,512,512]{2,1,0:T(8,128)(2,1)} %param.10) | copy-start | bytes 1572868
  91.6 14.5 %copy-start.4 = (s32[1,8,8]{2,1,0:T(8,128)S(1)}, s32[1,8,8]{2,1,0:T(8,128)}, u32[]{:S(2)}) copy-start(s32[1,8,8]{2,1,0:T(8,128)} %param.11) | copy-start | bytes 772
  91.6 65.3 %all-to-all-start = ((bf16[64,32,512]{2,1,0:T(8,128)(2,1)}), bf16[64,32,512]{2,1,0:T(8,128)(2,1)S(1)}, u32[]{:S(2)}, u32[]{:S(2)}) async-start(bf16[64,32,512]{2,1,0:T(8,128)(2,1)} %bitcast.12), calls=%async_computation | async-start | bytes 4194304 | tf_op jit(solution)/shard_map/all_to_all | solution.py:42
  159.6 55.4 %all-to-all-start.1 = ((bf16[64,32,512]{2,1,0:T(8,128)(2,1)}), bf16[64,32,512]{2,1,0:T(8,128)(2,1)S(1)}, u32[]{:S(2)}, u32[]{:S(2)}) async-start(bf16[64,32,512]{2,1,0:T(8,128)(2,1)} %convolution_convert_fusion), calls=%async_computation.1 | async-start | bytes 4194304 | tf_op jit(solution)/shard_map/all_to_all | solution.py:47
where the time goes:
time: 220 us
  waiting for transfers between devices  150 us (68%)
  starting transfers between devices  27 us (12%)
  other arithmetic  19.1 us (9%)
  local copies, waits for them, and re-layouts  13.2 us (6%)
  matrix products  10.9 us (5%)
    all_to_all x1, waiting for transfers between devices, local(): lax.all_to_all(result, 'leaf', split_axis=0, concat_axis=0, tiled=True)  50.7 us
    all_to_all x1, waiting for transfers between devices, local(): lax.all_to_all(sectioned, 'leaf', split_axis=0, concat_axis=0, tiled=True)  50.5 us
    ppermute x3, waiting for transfers between devices, swapped(): return lax.ppermute(value, axis, pairs)  48.4 us
    another operation x3, other arithmetic  18.2 us
    all_to_all x1, starting transfers between devices, local(): lax.all_to_all(sectioned, 'leaf', split_axis=0, concat_axis=0, tiled=True)  14.3 us
    ppermute x3, starting transfers between devices, swapped(): return lax.ppermute(value, axis, pairs)  8.07 us
    scatter x1, local copies, waits for them, and re-layouts, local(): jnp.zeros((leaves * capacity, features), jnp.bfloat16).at[position]  6.7 us
    gather x1, local copies, waits for them, and re-layouts, local(): return returned[position]  5.07 us
  transfers between devices with their start and end apart: 5, of which 5 were waited for; matrix products, arithmetic and copies ran while one was open for 10% of the time, Pallas kernels for 0%

commit v1 on v0

v1 whole, which is shorter than its diff:
```python
import jax
import jax.numpy as jnp
from jax import lax
from jax.experimental import pallas as pl
from jax.experimental.pallas import tpu as pltpu
from jax.sharding import PartitionSpec as P

BS = 64
LEVELS = 3
EPS = 1e-06
CHUNKS = 8
PIECES = 2
F32, BF16, I32 = jnp.float32, jnp.bfloat16, jnp.int32


def leaf_of(y, x, zh, c):
    return ((lax.rem(y + 4, 4) * 4 + lax.rem(x + 4, 4)) * 2 + zh) * 2 + c


def kernel(x_ref, own_col, own_row, keep, sib, coup, pat, out_ref,
           twin, cur1, far, cur2, side, cur3, wall, packed, rbuf, res, ret, pmat, umat, acc,
           twin_s, twin_r, far_s, far_r, side_s, side_r, zc_s, zc_r, g_s, g_r, d_s, d_r, b_s, b_r):
    rows, modes = x_ref.shape
    size = rows // CHUNKS
    leaf, zl = lax.axis_index("leaf"), lax.axis_index("blk")
    c, zh = lax.rem(leaf, 2), lax.rem(leaf // 2, 2)
    x, y = lax.rem(leaf // 4, 4), leaf // 16
    z = zh * 4 + zl

    def at(dy=0, dx=0, core=None):
        return (leaf_of(y + dy, x + dx, zh, c if core is None else core), zl)

    def at_z(dz):
        t = lax.rem(z + dz + 8, 8)
        return (leaf_of(y, x, t // 4, c), lax.rem(t, 4))

    twin_dev = at(core=1 - c)
    far_dev = at_z(4)
    side_dev = at(dx=1 - 2 * lax.rem(x, 2))
    skip_dev = at(dy=2)
    knight_dev = at(dy=1, dx=2)
    unknight_dev = at(dy=-1, dx=2)
    around = [at(dx=1, core=s) for s in range(2)] + [at(dx=-1, core=s) for s in range(2)]
    around += [at(dy=1, core=s) for s in range(2)] + [at(dy=-1, core=s) for s in range(2)]
    peers = [twin_dev, far_dev, at_z(1), at_z(-1), skip_dev, knight_dev, unknight_dev] + around

    barrier = pltpu.get_barrier_semaphore()
    for peer in peers:
        pl.semaphore_signal(barrier, inc=1, device_id=peer, device_id_type=pl.DeviceIdType.MESH)
    pl.semaphore_wait(barrier, len(peers))

    sends = []

    def send(src, dst, ss, rs, dev):
        copy = pltpu.make_async_remote_copy(
            src_ref=src, dst_ref=dst, send_sem=ss, recv_sem=rs,
            device_id=dev, device_id_type=pl.DeviceIdType.MESH)
        copy.start()
        sends.append(copy)

    def arrived(dst, ss, rs, dev):
        pltpu.make_async_remote_copy(
            src_ref=dst, dst_ref=dst, send_sem=ss, recv_sem=rs,
            device_id=dev, device_id_type=pl.DeviceIdType.MESH).wait_recv()

    def part(i):
        return pl.ds(i * size, size)

    for i in range(CHUNKS):
        send(x_ref.at[part(i)], twin.at[part(i)], twin_s.at[i], twin_r.at[i], twin_dev)

    grid_r = lax.broadcasted_iota(I32, (modes, 8), 0) // BS
    grid_c = lax.broadcasted_iota(I32, (modes, 8), 1)
    spread = (grid_r == grid_c).astype(F32).astype(BF16)
    wide_r = lax.broadcasted_iota(I32, (8, modes), 0)
    wide_c = lax.broadcasted_iota(I32, (8, modes), 1) // BS
    spread_t = (wide_r == wide_c).astype(F32).astype(BF16)
    half = jnp.dot(spread, pat[0].astype(F32).astype(BF16), preferred_element_type=F32).astype(BF16)
    mask = jnp.dot(half, spread_t, preferred_element_type=F32).astype(BF16)
    mine, other = y * 2 + zh, y * 2 + (1 - zh)
    wall[mine] = coup[0] * mask

    up = 1 - 2 * c
    step = jnp.where(c == 0, zl, 3 - zl)
    next_dev, prev_dev = at_z(up), at_z(-up)
    deep = modes // PIECES
    chain_slot = jnp.where(step == 3, mine, other)

    def chain(p):
        piece = wall.at[chain_slot, pl.ds(p * deep, deep)]
        return pltpu.make_async_remote_copy(
            src_ref=piece, dst_ref=piece, send_sem=zc_s.at[p], recv_sem=zc_r.at[p],
            device_id=next_dev, device_id_type=pl.DeviceIdType.MESH)

    def chain_arrived(p):
        arrived(wall.at[other, pl.ds(p * deep, deep)], zc_s.at[p], zc_r.at[p], prev_dev)

    @pl.when(step == 3)
    def _():
        for p in range(PIECES):
            chain(p).start()

    def gather_send(slot, n, dev):
        send(wall.at[slot], wall.at[slot], g_s.at[n], g_r.at[n], dev)

    def gather_arrived(slot, n, dev):
        arrived(wall.at[slot], g_s.at[n], g_r.at[n], dev)

    y2, yn, yp = lax.rem(y + 2, 4), lax.rem(y + 3, 4), lax.rem(y + 1, 4)
    gather_send(mine, 0, skip_dev)
    gather_send(mine, 1, knight_dev)

    def level(l, mine_ref, other_ref, dst, i):
        total = jnp.dot(mine_ref[part(i)], keep[l], preferred_element_type=F32)
        total = total + jnp.dot(other_ref[part(i)], sib[l], preferred_element_type=F32)
        scale = lax.rsqrt(jnp.mean(total * total, axis=1, keepdims=True) + EPS)
        dst[part(i)] = (total * scale).astype(BF16)

    for i in range(CHUNKS):
        arrived(twin.at[part(i)], twin_s.at[i], twin_r.at[i], twin_dev)
        level(0, x_ref, twin, cur1, i)
        send(cur1.at[part(i)], far.at[part(i)], far_s.at[i], far_r.at[i], far_dev)

    colour = lax.rem(x + 2 * lax.rem(y, 2), 4)

    def base_of(o):
        oc, ozh, ox, oy = o & 1, (o >> 1) & 1, (o >> 2) & 3, o >> 4
        rel = (ox + 2 * (oy & 1) - colour + 4) & 3
        return ((((oy >> 1) * 4 + rel) * 2 + oc) * 4 + (oy & 1) * 2 + ozh) * 32

    tri_r = lax.broadcasted_iota(I32, (rows, rows), 0)
    tri_c = lax.broadcasted_iota(I32, (rows, rows), 1)
    pmat[0] = (tri_c < tri_r).astype(F32).astype(BF16)
    pmat[1] = (tri_r < tri_c).astype(F32).astype(BF16)
    hot = (own_col[...] == lax.broadcasted_iota(I32, (rows, 128), 1)).astype(F32)
    rank = jnp.sum(jnp.dot(pmat[0], hot.astype(BF16), preferred_element_type=F32) * hot, axis=1, keepdims=True)
    pos_col = base_of(own_col[...]) + rank.astype(I32)
    hot = (own_row[...] == lax.broadcasted_iota(I32, (128, rows), 0)).astype(F32)
    rank = jnp.sum(jnp.dot(hot.astype(BF16), pmat[1], preferred_element_type=F32) * hot, axis=0, keepdims=True)
    pos_row = base_of(own_row[...]) + rank.astype(I32)
    for h in range(2):
        pmat[h] = (tri_r + h * rows == pos_row).astype(F32).astype(BF16)
        umat[h] = (tri_c + h * rows == pos_col).astype(F32).astype(BF16)

    for p in range(PIECES):
        @pl.when(step < 3)
        def _():
            chain_arrived(p)
            chain(p).start()

    def level2(i):
        arrived(side.at[part(i)], side_s.at[i], side_r.at[i], side_dev)
        level(2, cur2, side, cur3, i)

    for i in range(CHUNKS):
        arrived(far.at[part(i)], far_s.at[i], far_r.at[i], far_dev)
        level(1, cur1, far, cur2, i)
        send(cur2.at[part(i)], side.at[part(i)], side_s.at[i], side_r.at[i], side_dev)
        if i:
            level2(i - 1)
        if i == 2:
            @pl.when(step == 3)
            def _():
                for p in range(PIECES):
                    chain_arrived(p)
            gather_send(other, 2, skip_dev)
            gather_send(other, 3, knight_dev)
        if i == 4:
            gather_arrived(yn * 2 + zh, 1, unknight_dev)
            gather_send(yn * 2 + zh, 4, skip_dev)
        if i == 6:
            gather_arrived(yn * 2 + (1 - zh), 3, unknight_dev)
            gather_send(yn * 2 + (1 - zh), 5, skip_dev)
    level2(CHUNKS - 1)

    def block(ref, h, rel, core):
        return ref.at[pl.ds(((h * 4 + rel) * 2 + core) * 128, 128)]

    def source(h, n):
        if n == 1:
            return twin_dev
        if n < 4:
            return at(dx=-1, core=n - 2)
        if n < 6:
            return at(dx=1, core=n - 4)
        return at(dy=-1 if h == 0 else 1, core=n - 6)

    for h in range(2):
        for rel in (1, 3, 2, 0):
            first = (h * 4 + rel) * 256
            packed[pl.ds(first, 256)] = jnp.dot(
                pmat[h, pl.ds(rel * 256, 256), :], cur3[...], preferred_element_type=F32).astype(BF16)
            if rel == 0:
                rbuf[h, 0] = packed[pl.ds(first + c * 128, 128)]
                send(block(packed, h, 0, 1 - c), rbuf.at[h, 1], d_s.at[h, 1], d_r.at[h, 1], twin_dev)
                continue
            place = {1: 2, 3: 4, 2: 6}[rel]
            for s in range(2):
                dev = {1: at(dx=1, core=s), 3: at(dx=-1, core=s), 2: at(dy=1 if h == 0 else -1, core=s)}[rel]
                send(block(packed, h, rel, s), rbuf.at[h, place + c], d_s.at[h, place + s], d_r.at[h, place + c], dev)

    gather_arrived(y2 * 2 + zh, 0, skip_dev)
    gather_arrived(y2 * 2 + (1 - zh), 2, skip_dev)
    gather_arrived(yp * 2 + zh, 4, skip_dev)
    gather_arrived(yp * 2 + (1 - zh), 5, skip_dev)

    for h in range(2):
        for n in range(1, 8):
            arrived(rbuf.at[h, n], d_s.at[h, n], d_r.at[h, n], source(h, n))
        for e in range(4):
            lines = pl.ds(e * 32, 32)
            product = jnp.dot(rbuf[h, :, lines, :].reshape(256, modes), wall[h * 4 + e], preferred_element_type=F32)
            res[h, :, lines, :] = product.astype(BF16).reshape(8, 32, modes)
        for n, rel in ((2, 1), (3, 1), (4, 3), (5, 3), (6, 2), (7, 2), (1, 0)):
            send(res.at[h, n], block(ret, h, rel, c), b_s.at[h, n],
                 b_r.at[h, 1 if rel == 0 else rel * 2 + c], source(h, n))
        ret[pl.ds(h * 1024 + c * 128, 128)] = res[h, 0]

    for h in range(2):
        arrived(block(ret, h, 0, 1 - c), b_s.at[h, 1], b_r.at[h, 1], twin_dev)
        for rel in (1, 3, 2):
            for s in range(2):
                dev = {1: at(dx=1, core=s), 3: at(dx=-1, core=s), 2: at(dy=1 if h == 0 else -1, core=s)}[rel]
                arrived(block(ret, h, rel, s), b_s.at[h, rel * 2 + s], b_r.at[h, rel * 2 + s], dev)
        got = jnp.dot(umat[h], ret[pl.ds(h * 1024, 1024)], preferred_element_type=F32)
        if h == 0:
            acc[...] = got
        else:
            out_ref[...] = (acc[...] + got).astype(BF16)

    for copy in sends:
        copy.wait_send()
    for p in range(PIECES):
        chain(p).wait_send()


def local(interface, owners, keep_proj, sibling_proj, coupling, pattern):
    rows, modes = interface.shape
    vmem = pl.BlockSpec(memory_space=pltpu.VMEM)
    dma = pltpu.SemaphoreType.DMA
    return pl.pallas_call(
        kernel,
        out_shape=jax.ShapeDtypeStruct((rows, modes), BF16),
        in_specs=[vmem] * 7,
        out_specs=vmem,
        scratch_shapes=[pltpu.VMEM((rows, modes), BF16)] * 6
        + [
            pltpu.VMEM((8, modes, modes), BF16),
            pltpu.VMEM((2 * rows, modes), BF16),
            pltpu.VMEM((2, 8, 128, modes), BF16),
            pltpu.VMEM((2, 8, 128, modes), BF16),
            pltpu.VMEM((2 * rows, modes), BF16),
            pltpu.VMEM((2, rows, rows), BF16),
            pltpu.VMEM((2, rows, rows), BF16),
            pltpu.VMEM((rows, modes), F32),
        ]
        + [dma((CHUNKS,))] * 6
        + [dma((PIECES,))] * 2
        + [dma((6,))] * 2
        + [dma((2, 8))] * 4,
        compiler_params=pltpu.CompilerParams(
            collective_id=0, has_side_effects=True, vmem_limit_bytes=60 << 20),
        name="condense",
    )(interface, owners, owners.reshape(1, rows), keep_proj, sibling_proj, coupling, pattern)


def solution(mesh):
    in_specs = (
        P(("leaf", "blk"), None),
        P(("leaf", "blk"), None),
        P(),
        P(),
        P("leaf", None, None),
        P("leaf", None, None),
    )
    out_specs = P(("leaf", "blk"), None)
    return jax.shard_map(local, mesh=mesh, in_specs=in_specs, out_specs=out_specs, check_vma=False)
```

time: 220 us -> 152 us (0.69)
  waiting for transfers between devices: 150 us -> 0 us
  Pallas kernels: 0 us -> 147 us
  starting transfers between devices: 27 us -> 0 us
  other arithmetic: 19.1 us -> 0 us
  matrix products: 10.9 us -> 0 us
  local copies, waits for them, and re-layouts: 13.2 us -> 3.97 us
    pallas_call x0 -> x1, Pallas kernels: none -> 147 us  [local(): pl.pallas_call(kernel, out_shape=jax.ShapeDtypeStruct((rows, modes), BF16...]
    all_to_all x2 -> x0, waiting for transfers between devices: 101 us -> none  [the longest x1 50.7 us: local(): lax.all_to_all(result, 'leaf', split_axis=0, concat_axis=0, tiled=True)]
    ppermute x3 -> x0, waiting for transfers between devices: 48.4 us -> none  [swapped(): return lax.ppermute(value, axis, pairs)]
    all_to_all x2 -> x0, starting transfers between devices: 18.9 us -> none  [the longest x1 14.3 us: local(): lax.all_to_all(sectioned, 'leaf', split_axis=0, concat_axis=0, tiled=True)]
    another operation x3 -> x0, other arithmetic: 18.2 us -> none
    dot_general x7 -> x0, matrix products: 10.9 us -> none  [the longest x3 4.64 us: local(): jnp.dot(sibling, sibling_proj[tree_level], preferred_element_type=jnp.flo...]
    ppermute x3 -> x0, starting transfers between devices: 8.07 us -> none  [swapped(): return lax.ppermute(value, axis, pairs)]
    scatter x1 -> x0, local copies, waits for them, and re-layouts: 6.7 us -> none  [local(): jnp.zeros((leaves * capacity, features), jnp.bfloat16).at[position]]
  transfers between devices with their start and end apart: 5 -> 0, of which waited for: 5 -> 0; matrix products, arithmetic and copies ran while one was open for 10% -> 0% of each run, Pallas kernels for 0% -> 0%
where the time goes in v1:
time: 152 us; the launch traced here: 151 us
  Pallas kernels  147 us (97%)
  local copies, waits for them, and re-layouts  3.97 us (3%)
    pallas_call x1, Pallas kernels, local(): pl.pallas_call(kernel, out_shape=jax.ShapeDtypeStruct((rows, modes), BF16...  147 us
    unnamed x2, local copies, waits for them, and re-layouts  3.97 us

profile of v1, /device:TPU:33, one launch (start us, length us, event | category | flops | bytes accessed | tf_op | source)
XLA Modules:
  0.0 151.0 jit_solution(2065926704351484632)
XLA Ops:
  0.0 1.7 %copy.7.own_col = s32[1024,1]{1,0:T(8,128)} copy(s32[1024,1]{0,1:T(1,128)} %param.7) | data formatting | bytes 8192 | tf_op args[1]
  1.7 147.0 %condense.1 = bf16[1024,512]{1,0:T(8,128)(2,1)} custom-call(bf16[1024,512]{1,0:T(8,128)(2,1)} %x_ref.1, s32[1024,1]{1,0:T(8,128)} %copy.7.own_col, s32[1,1024]{1,0:T(1,128)} %bitcast.1, bf16[3,512,512]{2,1,0:T(8,128)(2,1)} %keep.1, bf16[3,512,512]{2,1,0:T(8,128)(2,1)} %sib.1, bf16[1,512,512]{2,1,0:T(8,128)(2,1)} %coup.1, s32[1,8,8]{2,1,0:T(8,128)} %pat.1), custom_call_target="tpu_custom_call" | custom-call | tf_op jit(solution)/shard_map/condense/pallas_call | solution.py:241
  148.7 2.3 %copy.9 = bf16[1024,512]{1,0:T(8,128)(2,1)} copy(bf16[1024,512]{1,0:T(8,128)(2,1)} %condense.1) | data formatting | bytes 2097152

commit v2 on v0

v2 whole, which is shorter than its diff:
```python
import jax
import jax.numpy as jnp
from jax import lax
from jax.experimental import pallas as pl
from jax.experimental.pallas import tpu as pltpu
from jax.sharding import PartitionSpec as P

BS = 64
LEVELS = 3
EPS = 1e-06
CHUNKS = 8
PIECES = 4
METER = False
F32, BF16, I32 = jnp.float32, jnp.bfloat16, jnp.int32


REACH = (
    ((0, 0), (0, 0)),
    ((2, 0), (0, 2)),
    ((1, 1), (-1, -1)),
    ((-1, 1), (1, -1)),
    ((1, 0), (1, 0)),
    ((-1, 0), (-1, 0)),
    ((0, 1), (0, 1)),
    ((0, -1), (0, -1)),
)


def leaf_of(y, x, zh, c):
    return ((lax.rem(y + 4, 4) * 4 + lax.rem(x + 4, 4)) * 2 + zh) * 2 + c


def kernel(x_ref, own_row, keep, sib, coup, pat, out_ref,
           twin, cur1, far, cur2, side, cur3, wall, packed, rbuf, res, ret, pmat, umat, acc, pos,
           twin_s, twin_r, far_s, far_r, side_s, side_r, zc_s, zc_r, g_s, g_r, d_s, d_r, b_s, b_r):
    rows, modes = x_ref.shape
    size = rows // CHUNKS
    leaf, zl = lax.axis_index("leaf"), lax.axis_index("blk")
    c, zh = lax.rem(leaf, 2), lax.rem(leaf // 2, 2)
    x, y = lax.rem(leaf // 4, 4), leaf // 16
    z = zh * 4 + zl

    def at(dx=0, dy=0, core=None):
        return (leaf_of(y + dy, x + dx, zh, c if core is None else core), zl)

    def at_z(dz):
        t = lax.rem(z + dz + 8, 8)
        return (leaf_of(y, x, t // 4, c), lax.rem(t, 4))

    twin_dev = at(core=1 - c)
    far_dev = at_z(4)
    side_dev = at(dx=1 - 2 * lax.rem(x, 2))
    pair_dev = at(2, 2)
    peers = [twin_dev, far_dev, at_z(1), at_z(-1), pair_dev]
    near = ((2, 0), (0, 2), (1, 1), (-1, -1), (-1, 1), (1, -1), (1, 0), (-1, 0), (0, 1), (0, -1))
    peers += [at(dx, dy, s) for dx, dy in near for s in range(2)]

    barrier = pltpu.get_barrier_semaphore()
    for peer in peers:
        pl.semaphore_signal(barrier, inc=1, device_id=peer, device_id_type=pl.DeviceIdType.MESH)
    pl.semaphore_wait(barrier, len(peers))

    sends = []

    def send(src, dst, ss, rs, dev):
        copy = pltpu.make_async_remote_copy(
            src_ref=src, dst_ref=dst, send_sem=ss, recv_sem=rs,
            device_id=dev, device_id_type=pl.DeviceIdType.MESH)
        copy.start()
        sends.append(copy)

    def arrived(dst, ss, rs, dev):
        pltpu.make_async_remote_copy(
            src_ref=dst, dst_ref=dst, send_sem=ss, recv_sem=rs,
            device_id=dev, device_id_type=pl.DeviceIdType.MESH).wait_recv()

    def part(i):
        return pl.ds(i * size, size)

    for i in range(CHUNKS):
        send(x_ref.at[part(i)], twin.at[part(i)], twin_s.at[i], twin_r.at[i], twin_dev)

    def level(l, mine_ref, other_ref, dst, i):
        total = jnp.dot(mine_ref[part(i)], keep[l], preferred_element_type=F32)
        total = total + jnp.dot(other_ref[part(i)], sib[l], preferred_element_type=F32)
        scale = lax.rsqrt(jnp.mean(total * total, axis=1, keepdims=True) + EPS)
        dst[part(i)] = (total * scale).astype(BF16)

    def far_send(i):
        send(cur1.at[part(i)], far.at[part(i)], far_s.at[i], far_r.at[i], far_dev)

    for i in range(CHUNKS):
        arrived(twin.at[part(i)], twin_s.at[i], twin_r.at[i], twin_dev)
        level(0, x_ref, twin, cur1, i)
        far_send(i)

    grid_r = lax.broadcasted_iota(I32, (modes, 8), 0) // BS
    grid_c = lax.broadcasted_iota(I32, (modes, 8), 1)
    spread = (grid_r == grid_c).astype(F32).astype(BF16)
    wide_r = lax.broadcasted_iota(I32, (8, modes), 0)
    wide_c = lax.broadcasted_iota(I32, (8, modes), 1) // BS
    spread_t = (wide_r == wide_c).astype(F32).astype(BF16)
    half = jnp.dot(spread, pat[0].astype(F32).astype(BF16), preferred_element_type=F32).astype(BF16)
    mask = jnp.dot(half, spread_t, preferred_element_type=F32).astype(BF16)
    upper = y // 2
    wall[upper] = coup[0] * mask
    send(wall.at[upper], wall.at[upper], g_s.at[0], g_r.at[0], pair_dev)

    up = 1 - 2 * c
    step = jnp.where(c == 0, zl, 3 - zl)
    next_dev, prev_dev = at_z(up), at_z(-up)
    deep = modes // PIECES

    def chain(n):
        col, p = n // PIECES, n % PIECES
        piece = pl.ds(p * deep, deep)
        return pltpu.make_async_remote_copy(
            src_ref=wall.at[jnp.where(step == 3, 0, 2) + col, piece], dst_ref=wall.at[2 + col, piece],
            send_sem=zc_s.at[n], recv_sem=zc_r.at[n],
            device_id=next_dev, device_id_type=pl.DeviceIdType.MESH)

    def chain_arrived(n):
        arrived(wall.at[2 + n // PIECES, pl.ds(n % PIECES * deep, deep)], zc_s.at[n], zc_r.at[n], prev_dev)

    def base_of(o):
        oc, ozh, ox, oy = o & 1, (o >> 1) & 1, (o >> 2) & 3, o >> 4
        dy = (oy - y + 4) & 3
        dx = (ox - x + 4 + (dy & 2)) & 3
        dy = dy & 1
        place = ((dx + dy) & 1) * 4 + dy * 2 + (dx >> 1)
        return ((((ozh ^ zh) * 8 + place) * 2 + oc) * 2 + (oy >> 1)) * 32

    tri_r = lax.broadcasted_iota(I32, (rows, rows), 0)
    tri_c = lax.broadcasted_iota(I32, (rows, rows), 1)

    def prepare(n):
        if n == 0:
            umat[0] = (tri_r < tri_c).astype(F32).astype(BF16)
            hot = (own_row[...] == lax.broadcasted_iota(I32, (64, rows), 0)).astype(F32)
            rank = jnp.sum(jnp.dot(hot.astype(BF16), umat[0], preferred_element_type=F32) * hot, axis=0, keepdims=True)
            pos[...] = base_of(own_row[...]) + rank.astype(I32)
        elif n < 3:
            pmat[n - 1] = (tri_r + (n - 1) * rows == pos[...]).astype(F32).astype(BF16)
        else:
            line = jnp.where(tri_r == tri_c, pos[...], 0)
            column = jnp.sum(line.astype(F32), axis=1, keepdims=True).astype(I32)
            umat[n - 3] = (tri_c + (n - 3) * rows == column).astype(F32).astype(BF16)

    def level2(i):
        arrived(side.at[part(i)], side_s.at[i], side_r.at[i], side_dev)
        level(2, cur2, side, cur3, i)

    def relay(col):
        @pl.when(step < 3)
        def _():
            for p in range(PIECES):
                chain_arrived(col * PIECES + p)
                chain(col * PIECES + p).start()

    for i in range(CHUNKS):
        arrived(far.at[part(i)], far_s.at[i], far_r.at[i], far_dev)
        if i == CHUNKS - 1:
            arrived(wall.at[1 - upper], g_s.at[0], g_r.at[0], pair_dev)

            @pl.when(step == 3)
            def _():
                for n in range(2 * PIECES):
                    chain(n).start()
        level(1, cur1, far, cur2, i)
        send(cur2.at[part(i)], side.at[part(i)], side_s.at[i], side_r.at[i], side_dev)
        if i:
            level2(i - 1)
        if i < 5:
            prepare(i)
    level2(CHUNKS - 1)

    def block(ref, g, q, core):
        return ref.at[pl.ds(((g * 8 + q) * 2 + core) * 64, 64)]

    def source(q, s):
        dx, dy = REACH[q][0]
        ex, ey = REACH[q][1]
        return at(jnp.where(c == 0, -dx, -ex), jnp.where(c == 0, -dy, -ey), s)

    def number(g, q, s):
        return (g * 8 + q) * 2 + s

    def rows_send(g, q):
        if q == 0:
            send(block(packed, g, 0, 1 - c), rbuf.at[g, 0, 0], d_s.at[g * 16], d_r.at[g * 16], twin_dev)
            return
        for s in range(2):
            send(block(packed, g, q, s), rbuf.at[g, q, c],
                 d_s.at[number(g, q, s)], d_r.at[number(g, q, c)], at(*REACH[q][s], s))

    def pack(g, k):
        packed[pl.ds(g * 1024 + k * 256, 256)] = jnp.dot(
            pmat[g, pl.ds(k * 256, 256), :], cur3[...], preferred_element_type=F32).astype(BF16)
        if k == 0:
            rbuf[g, 0, 1] = packed[pl.ds(g * 1024 + c * 64, 64)]

    def rows_arrived(g, q):
        if q == 0:
            arrived(rbuf.at[g, 0, 0], d_s.at[g * 16], d_r.at[g * 16], twin_dev)
            return
        for s in range(2):
            n = number(g, q, s)
            arrived(rbuf.at[g, q, s], d_s.at[n], d_r.at[n], source(q, s))

    def couple(g):
        for e in range(2):
            lines = pl.ds(e * 32, 32)
            left = rbuf[g, :, :, lines, :].reshape(512, modes)
            product = jnp.dot(left, wall[g * 2 + e], preferred_element_type=F32)
            res[g, :, :, lines, :] = product.astype(BF16).reshape(8, 2, 32, modes)

    def result_send(g, q):
        if q == 0:
            send(res.at[g, 0, 0], block(ret, g, 0, c), b_s.at[g * 16], b_r.at[g * 16], twin_dev)
            ret[pl.ds(g * 1024 + c * 64, 64)] = res[g, 0, 1]
            return
        for s in range(2):
            send(res.at[g, q, s], block(ret, g, q, c), b_s.at[number(g, q, s)], b_r.at[number(g, q, c)], source(q, s))

    def result_arrived(g, q):
        if q == 0:
            arrived(block(ret, g, 0, 1 - c), b_s.at[g * 16], b_r.at[g * 16], twin_dev)
            return
        for s in range(2):
            n = number(g, q, s)
            arrived(block(ret, g, q, s), b_s.at[n], b_r.at[n], at(*REACH[q][s], s))

    for g in range(2):
        for k in range(4):
            pack(g, k)
            if g == 0 or not METER:
                for q in (2 * k + 1, 2 * k):
                    rows_send(g, q)
        relay(g)
    for q in range(8):
        rows_arrived(0, q)
    if METER:
        for q in (1, 2, 3, 4, 5, 6, 7, 0):
            rows_send(1, q)
    couple(0)
    for q in (1, 2, 3, 4, 5, 6, 7, 0):
        result_send(0, q)

    @pl.when(step == 3)
    def _():
        for n in range(2 * PIECES):
            chain_arrived(n)
    for q in range(8):
        rows_arrived(1, q)
    couple(1)
    for q in (1, 2, 3, 4, 5, 6, 7, 0):
        result_send(1, q)
    for q in range(8):
        result_arrived(0, q)
    acc[...] = jnp.dot(umat[0], ret[pl.ds(0, 1024)], preferred_element_type=F32)
    for q in range(8):
        result_arrived(1, q)
    got = jnp.dot(umat[1], ret[pl.ds(1024, 1024)], preferred_element_type=F32)
    out_ref[...] = (acc[...] + got).astype(BF16)

    for copy in sends:
        copy.wait_send()
    for n in range(2 * PIECES):
        chain(n).wait_send()


def local(interface, owners, keep_proj, sibling_proj, coupling, pattern):
    rows, modes = interface.shape
    vmem = pl.BlockSpec(memory_space=pltpu.VMEM)
    dma = pltpu.SemaphoreType.DMA
    return pl.pallas_call(
        kernel,
        out_shape=jax.ShapeDtypeStruct((rows, modes), BF16),
        in_specs=[vmem] * 6,
        out_specs=vmem,
        scratch_shapes=[pltpu.VMEM((rows, modes), BF16)] * 6
        + [
            pltpu.VMEM((4, modes, modes), BF16),
            pltpu.VMEM((2 * rows, modes), BF16),
            pltpu.VMEM((2, 8, 2, 64, modes), BF16),
            pltpu.VMEM((2, 8, 2, 64, modes), BF16),
            pltpu.VMEM((2 * rows, modes), BF16),
            pltpu.VMEM((2, rows, rows), BF16),
            pltpu.VMEM((2, rows, rows), BF16),
            pltpu.VMEM((rows, modes), F32),
            pltpu.VMEM((1, rows), I32),
        ]
        + [dma((CHUNKS,))] * 6
        + [dma((2 * PIECES,))] * 2
        + [dma((1,))] * 2
        + [dma((32,))] * 4,
        compiler_params=pltpu.CompilerParams(
            collective_id=0, has_side_effects=True, vmem_limit_bytes=60 << 20),
        name="condense",
    )(interface, owners.reshape(1, rows), keep_proj, sibling_proj, coupling, pattern)


def solution(mesh):
    in_specs = (
        P(("leaf", "blk"), None),
        P(("leaf", "blk"), None),
        P(),
        P(),
        P("leaf", None, None),
        P("leaf", None, None),
    )
    out_specs = P(("leaf", "blk"), None)
    return jax.shard_map(local, mesh=mesh, in_specs=in_specs, out_specs=out_specs, check_vma=False)
```

time: 220 us -> 107 us (0.49)
  waiting for transfers between devices: 150 us -> 0 us
  Pallas kernels: 0 us -> 103 us
  starting transfers between devices: 27 us -> 0 us
  other arithmetic: 19.1 us -> 0 us
  local copies, waits for them, and re-layouts: 13.2 us -> 2.26 us
  matrix products: 10.9 us -> 0 us
    pallas_call x0 -> x1, Pallas kernels: none -> 103 us  [local(): pl.pallas_call(kernel, out_shape=jax.ShapeDtypeStruct((rows, modes), BF16...]
    all_to_all x2 -> x0, waiting for transfers between devices: 101 us -> none  [the longest x1 50.7 us: local(): lax.all_to_all(result, 'leaf', split_axis=0, concat_axis=0, tiled=True)]
    ppermute x3 -> x0, waiting for transfers between devices: 48.4 us -> none  [swapped(): return lax.ppermute(value, axis, pairs)]
    all_to_all x2 -> x0, starting transfers between devices: 18.9 us -> none  [the longest x1 14.3 us: local(): lax.all_to_all(sectioned, 'leaf', split_axis=0, concat_axis=0, tiled=True)]
    another operation x3 -> x0, other arithmetic: 18.2 us -> none
    dot_general x7 -> x0, matrix products: 10.9 us -> none  [the longest x3 4.64 us: local(): jnp.dot(sibling, sibling_proj[tree_level], preferred_element_type=jnp.flo...]
    ppermute x3 -> x0, starting transfers between devices: 8.07 us -> none  [swapped(): return lax.ppermute(value, axis, pairs)]
    scatter x1 -> x0, local copies, waits for them, and re-layouts: 6.7 us -> none  [local(): jnp.zeros((leaves * capacity, features), jnp.bfloat16).at[position]]
  transfers between devices with their start and end apart: 5 -> 0, of which waited for: 5 -> 0; matrix products, arithmetic and copies ran while one was open for 10% -> 0% of each run, Pallas kernels for 0% -> 0%
where the time goes in v2:
time: 107 us; the launch traced here: 105 us
  Pallas kernels  103 us (96%)
  local copies, waits for them, and re-layouts  2.26 us (2%)
    pallas_call x1, Pallas kernels, local(): pl.pallas_call(kernel, out_shape=jax.ShapeDtypeStruct((rows, modes), BF16...  103 us
    unnamed x1, local copies, waits for them, and re-layouts  2.26 us

profile of v2, /device:TPU:33, one launch (start us, length us, event | category | flops | bytes accessed | tf_op | source)
XLA Modules:
  0.0 104.9 jit_solution(9071541912918055236)
XLA Ops:
  0.0 102.6 %condense.1 = bf16[1024,512]{1,0:T(8,128)(2,1)} custom-call(bf16[1024,512]{1,0:T(8,128)(2,1)} %x_ref.1, s32[1,1024]{1,0:T(1,128)} %bitcast.1, bf16[3,512,512]{2,1,0:T(8,128)(2,1)} %keep.1, bf16[3,512,512]{2,1,0:T(8,128)(2,1)} %sib.1, bf16[1,512,512]{2,1,0:T(8,128)(2,1)} %coup.1, s32[1,8,8]{2,1,0:T(8,128)} %pat.1), custom_call_target="tpu_custom_call" | custom-call | tf_op jit(solution)/shard_map/condense/pallas_call | solution.py:276
  102.6 2.3 %copy.8 = bf16[1024,512]{1,0:T(8,128)(2,1)} copy(bf16[1024,512]{1,0:T(8,128)(2,1)} %condense.1) | data formatting | bytes 2097152

commit v3 on v2

--- a/solution.py
+++ b/solution.py
@@ -8,9 +8,9 @@
 BS = 64
 LEVELS = 3
 EPS = 1e-06
-CHUNKS = 8
+SIZES = (128, 128, 128, 128, 128, 128, 128, 64, 64)
+CHUNKS = len(SIZES)
 PIECES = 4
-METER = False
 F32, BF16, I32 = jnp.float32, jnp.bfloat16, jnp.int32
 
 
@@ -30,11 +30,10 @@
     return ((lax.rem(y + 4, 4) * 4 + lax.rem(x + 4, 4)) * 2 + zh) * 2 + c
 
 
-def kernel(x_ref, own_row, keep, sib, coup, pat, out_ref,
-           twin, cur1, far, cur2, side, cur3, wall, packed, rbuf, res, ret, pmat, umat, acc, pos,
+def kernel(x_hbm, own_hbm, keep_hbm, sib_hbm, coup_hbm, pat_hbm, out_ref,
+           x_ref, own_row, keep, sib, coup, pat, load_s, twin, cur1, far, cur2, side, cur3, wall, packed, rbuf, res, ret, pmat, umat, acc, pos,
            twin_s, twin_r, far_s, far_r, side_s, side_r, zc_s, zc_r, g_s, g_r, d_s, d_r, b_s, b_r):
-    rows, modes = x_ref.shape
-    size = rows // CHUNKS
+    rows, modes = x_hbm.shape
     leaf, zl = lax.axis_index("leaf"), lax.axis_index("blk")
     c, zh = lax.rem(leaf, 2), lax.rem(leaf // 2, 2)
     x, y = lax.rem(leaf // 4, 4), leaf // 16
@@ -58,6 +57,22 @@
     barrier = pltpu.get_barrier_semaphore()
     for peer in peers:
         pl.semaphore_signal(barrier, inc=1, device_id=peer, device_id_type=pl.DeviceIdType.MESH)
+
+    loads = {}
+
+    def load(name, src, dst):
+        loads[name] = pltpu.make_async_copy(src, dst, load_s.at[len(loads)])
+        loads[name].start()
+
+    load("x", x_hbm, x_ref)
+    load("keep0", keep_hbm.at[0], keep.at[0])
+    load("sib0", sib_hbm.at[0], sib.at[0])
+    load("coup", coup_hbm, coup)
+    load("pat", pat_hbm, pat)
+    load("own", own_hbm, own_row)
+    for l in (1, 2):
+        load(f"keep{l}", keep_hbm.at[l], keep.at[l])
+        load(f"sib{l}", sib_hbm.at[l], sib.at[l])
     pl.semaphore_wait(barrier, len(peers))
 
     sends = []
@@ -75,10 +90,10 @@
             device_id=dev, device_id_type=pl.DeviceIdType.MESH).wait_recv()
 
     def part(i):
-        return pl.ds(i * size, size)
+        return pl.ds(sum(SIZES[:i]), SIZES[i])
 
     for i in range(CHUNKS):
-        send(x_ref.at[part(i)], twin.at[part(i)], twin_s.at[i], twin_r.at[i], twin_dev)
+        send(x_hbm.at[part(i)], twin.at[part(i)], twin_s.at[i], twin_r.at[i], twin_dev)
 
     def level(l, mine_ref, other_ref, dst, i):
         total = jnp.dot(mine_ref[part(i)], keep[l], preferred_element_type=F32)
@@ -89,11 +104,15 @@
     def far_send(i):
         send(cur1.at[part(i)], far.at[part(i)], far_s.at[i], far_r.at[i], far_dev)
 
+    for name in ("x", "keep0", "sib0"):
+        loads[name].wait()
     for i in range(CHUNKS):
         arrived(twin.at[part(i)], twin_s.at[i], twin_r.at[i], twin_dev)
         level(0, x_ref, twin, cur1, i)
         far_send(i)
 
+    loads["coup"].wait()
+    loads["pat"].wait()
     grid_r = lax.broadcasted_iota(I32, (modes, 8), 0) // BS
     grid_c = lax.broadcasted_iota(I32, (modes, 8), 1)
     spread = (grid_r == grid_c).astype(F32).astype(BF16)
@@ -146,6 +165,9 @@
             column = jnp.sum(line.astype(F32), axis=1, keepdims=True).astype(I32)
             umat[n - 3] = (tri_c + (n - 3) * rows == column).astype(F32).astype(BF16)
 
+    for name in ("own", "keep1", "sib1", "keep2", "sib2"):
+        loads[name].wait()
+
     def level2(i):
         arrived(side.at[part(i)], side_s.at[i], side_r.at[i], side_dev)
         level(2, cur2, side, cur3, i)
@@ -233,15 +255,11 @@
     for g in range(2):
         for k in range(4):
             pack(g, k)
-            if g == 0 or not METER:
-                for q in (2 * k + 1, 2 * k):
-                    rows_send(g, q)
+            for q in (2 * k + 1, 2 * k):
+                rows_send(g, q)
         relay(g)
     for q in range(8):
         rows_arrived(0, q)
-    if METER:
-        for q in (1, 2, 3, 4, 5, 6, 7, 0):
-            rows_send(1, q)
     couple(0)
     for q in (1, 2, 3, 4, 5, 6, 7, 0):
         result_send(0, q)
@@ -258,9 +276,12 @@
     for q in range(8):
         result_arrived(0, q)
     acc[...] = jnp.dot(umat[0], ret[pl.ds(0, 1024)], preferred_element_type=F32)
-    for q in range(8):
+    for q in range(4, 8):
         result_arrived(1, q)
-    got = jnp.dot(umat[1], ret[pl.ds(1024, 1024)], preferred_element_type=F32)
+    acc[...] += jnp.dot(umat[1, :, 512:], ret[pl.ds(1536, 512)], preferred_element_type=F32)
+    for q in range(4):
+        result_arrived(1, q)
+    got = jnp.dot(umat[1, :, :512], ret[pl.ds(1024, 512)], preferred_element_type=F32)
     out_ref[...] = (acc[...] + got).astype(BF16)
 
     for copy in sends:
@@ -275,10 +296,19 @@
     dma = pltpu.SemaphoreType.DMA
     return pl.pallas_call(
         kernel,
-        out_shape=jax.ShapeDtypeStruct((rows, modes), BF16),
-        in_specs=[vmem] * 6,
+        out_shape=pltpu.VMEM((rows, modes), BF16),
+        in_specs=[pl.BlockSpec(memory_space=pltpu.HBM)] * 6,
         out_specs=vmem,
-        scratch_shapes=[pltpu.VMEM((rows, modes), BF16)] * 6
+        scratch_shapes=[
+            pltpu.VMEM((rows, modes), BF16),
+            pltpu.VMEM((1, rows), I32),
+            pltpu.VMEM(keep_proj.shape, BF16),
+            pltpu.VMEM(sibling_proj.shape, BF16),
+            pltpu.VMEM(coupling.shape, BF16),
+            pltpu.VMEM(pattern.shape, I32),
+            dma((10,)),
+        ]
+        + [pltpu.VMEM((rows, modes), BF16)] * 6
         + [
             pltpu.VMEM((4, modes, modes), BF16),
             pltpu.VMEM((2 * rows, modes), BF16),
@@ -295,7 +325,7 @@
         + [dma((1,))] * 2
         + [dma((32,))] * 4,
         compiler_params=pltpu.CompilerParams(
-            collective_id=0, has_side_effects=True, vmem_limit_bytes=60 << 20),
+            collective_id=0, has_side_effects=True, vmem_limit_bytes=56 << 20),
         name="condense",
     )(interface, owners.reshape(1, rows), keep_proj, sibling_proj, coupling, pattern)
 

time: 107 us -> 102 us (0.953)
  Pallas kernels: 103 us -> 100 us
  local copies, waits for them, and re-layouts: 2.26 us -> 0.97 us
    pallas_call x1, Pallas kernels: 103 us -> 100 us  [local(): pl.pallas_call(kernel, out_shape=pltpu.VMEM((rows, modes), BF16), in_spec...]
    unnamed x1, local copies, waits for them, and re-layouts: 2.26 us -> 0.97 us
where the time goes in v3:
time: 102 us; the launch traced here: 101 us
  Pallas kernels  100 us (98%)
    pallas_call x1, Pallas kernels, local(): pl.pallas_call(kernel, out_shape=pltpu.VMEM((rows, modes), BF16), in_spec...  100 us

profile of v3, /device:TPU:33, one launch (start us, length us, event | category | flops | bytes accessed | tf_op | source)
XLA Modules:
  0.0 101.0 jit_solution(18266926721991888718)
XLA Ops:
  0.0 100.0 %condense.1 = bf16[1024,512]{1,0:T(8,128)(2,1)S(1)} custom-call(bf16[1024,512]{1,0:T(8,128)(2,1)} %x_hbm.1, s32[1,1024]{1,0:T(1,128)} %bitcast.1, bf16[3,512,512]{2,1,0:T(8,128)(2,1)} %keep_hbm.1, bf16[3,512,512]{2,1,0:T(8,128)(2,1)} %sib_hbm.1, bf16[1,512,512]{2,1,0:T(8,128)(2,1)} %coup_hbm.1, s32[1,8,8]{2,1,0:T(8,128)} %pat_hbm.1), custom_call_target="tpu_custom_call" | custom-call | tf_op jit(solution)/shard_map/condense/pallas_call | solution.py:297
  100.0 1.0 copy.8

commit v4 on v3

--- a/solution.py
+++ b/solution.py
@@ -11,6 +11,14 @@
 SIZES = (128, 128, 128, 128, 128, 128, 128, 64, 64)
 CHUNKS = len(SIZES)
 PIECES = 4
+RELAY = (
+    ((0, 1), (), ()),
+    ((2, 3), (0, 1), ()),
+    ((4, 5), (2, 3), (0, 1)),
+    ((6, 7), (4, 5), (2, 3)),
+    ((), (6, 7), (4, 5)),
+    ((), (), (6, 7)),
+)
 F32, BF16, I32 = jnp.float32, jnp.bfloat16, jnp.int32
 
 
@@ -18,12 +26,20 @@
     ((0, 0), (0, 0)),
     ((2, 0), (0, 2)),
     ((1, 1), (-1, -1)),
-    ((-1, 1), (1, -1)),
+    ((1, -1), (-1, 1)),
     ((1, 0), (1, 0)),
     ((-1, 0), (-1, 0)),
     ((0, 1), (0, 1)),
     ((0, -1), (0, -1)),
 )
+SHARED = (
+    (1, 2, 0), (1, 3, 0), (1, 1, 0), (1, 4, 0), (1, 4, 1), (0, 0, 0), (0, 0, 1),
+    (2, 2, 1), (2, 3, 1), (2, 5, 0), (2, 5, 1), (3, 6, 0), (3, 6, 1),
+)
+BLOCKS = (
+    SHARED + ((3, 1, 1), (4, 7, 0), (4, 7, 1)),
+    SHARED + ((4, 7, 0), (4, 7, 1), (4, 1, 1)),
+)
 
 
 def leaf_of(y, x, zh, c):
@@ -31,7 +47,7 @@
 
 
 def kernel(x_hbm, own_hbm, keep_hbm, sib_hbm, coup_hbm, pat_hbm, out_ref,
-           x_ref, own_row, keep, sib, coup, pat, load_s, twin, cur1, far, cur2, side, cur3, wall, packed, rbuf, res, ret, pmat, umat, acc, pos,
+           x_ref, own_all, keep, sib, coup, pat, load_s, cur3x, wide, twin, cur1, far, cur2, side, cur3, wall, packed, rbuf, res, ret, pmat, umat, acc, pos, own_s, own_r, cast_s, cast_r,
            twin_s, twin_r, far_s, far_r, side_s, side_r, zc_s, zc_r, g_s, g_r, d_s, d_r, b_s, b_r):
     rows, modes = x_hbm.shape
     leaf, zl = lax.axis_index("leaf"), lax.axis_index("blk")
@@ -48,7 +64,9 @@
 
     twin_dev = at(core=1 - c)
     far_dev = at_z(4)
-    side_dev = at(dx=1 - 2 * lax.rem(x, 2))
+    hot = 1 - 2 * lax.rem(x, 2)
+    side_dev = at(dx=hot)
+    beside = (side_dev, at(dx=-hot), at(dy=-1), at(dy=1))
     pair_dev = at(2, 2)
     peers = [twin_dev, far_dev, at_z(1), at_z(-1), pair_dev]
     near = ((2, 0), (0, 2), (1, 1), (-1, -1), (-1, 1), (1, -1), (1, 0), (-1, 0), (0, 1), (0, -1))
@@ -69,7 +87,7 @@
     load("sib0", sib_hbm.at[0], sib.at[0])
     load("coup", coup_hbm, coup)
     load("pat", pat_hbm, pat)
-    load("own", own_hbm, own_row)
+    load("own", own_hbm, own_all.at[0])
     for l in (1, 2):
         load(f"keep{l}", keep_hbm.at[l], keep.at[l])
         load(f"sib{l}", sib_hbm.at[l], sib.at[l])
@@ -104,8 +122,10 @@
     def far_send(i):
         send(cur1.at[part(i)], far.at[part(i)], far_s.at[i], far_r.at[i], far_dev)
 
-    for name in ("x", "keep0", "sib0"):
+    for name in ("x", "keep0", "sib0", "own"):
         loads[name].wait()
+    for n, slot in enumerate((1, 2, 4, 3)):
+        send(own_all.at[0], own_all.at[slot], own_s.at[n], own_r.at[slot - 1], beside[n])
     for i in range(CHUNKS):
         arrived(twin.at[part(i)], twin_s.at[i], twin_r.at[i], twin_dev)
         level(0, x_ref, twin, cur1, i)
@@ -141,43 +161,59 @@
     def chain_arrived(n):
         arrived(wall.at[2 + n // PIECES, pl.ds(n % PIECES * deep, deep)], zc_s.at[n], zc_r.at[n], prev_dev)
 
-    def base_of(o):
+    def base_of(o, home_x, home_y, towards):
         oc, ozh, ox, oy = o & 1, (o >> 1) & 1, (o >> 2) & 3, o >> 4
-        dy = (oy - y + 4) & 3
-        dx = (ox - x + 4 + (dy & 2)) & 3
+        dy = (oy - home_y) & 3
+        dx = (towards * (ox - home_x) + (dy & 2)) & 3
         dy = dy & 1
-        place = ((dx + dy) & 1) * 4 + dy * 2 + (dx >> 1)
-        return ((((ozh ^ zh) * 8 + place) * 2 + oc) * 2 + (oy >> 1)) * 32
-
+        q = ((dx + dy) & 1) * 4 + dy * 2 + (dx >> 1)
+        return ((((ozh ^ zh) * 8 + q) * 2 + oc) * 2 + (oy >> 1)) * 32
+
+    homes = ((x, y, hot), (x + hot, y, -hot), (x - hot, y, -hot), (x, y - 1, hot), (x, y + 1, hot))
     tri_r = lax.broadcasted_iota(I32, (rows, rows), 0)
     tri_c = lax.broadcasted_iota(I32, (rows, rows), 1)
 
     def prepare(n):
         if n == 0:
             umat[0] = (tri_r < tri_c).astype(F32).astype(BF16)
-            hot = (own_row[...] == lax.broadcasted_iota(I32, (64, rows), 0)).astype(F32)
-            rank = jnp.sum(jnp.dot(hot.astype(BF16), umat[0], preferred_element_type=F32) * hot, axis=0, keepdims=True)
-            pos[...] = base_of(own_row[...]) + rank.astype(I32)
+            for k in range(5):
+                if k:
+                    arrived(own_all.at[k], own_s.at[k - 1], own_r.at[k - 1], beside[k - 1])
+                mine = own_all[k]
+                named = (mine == lax.broadcasted_iota(I32, (64, rows), 0)).astype(F32)
+                rank = jnp.dot(named.astype(BF16), umat[0], preferred_element_type=F32)
+                rank = jnp.sum(rank * named, axis=0, keepdims=True)
+                pos[k] = base_of(mine, *homes[k]) + rank.astype(I32)
         elif n < 3:
-            pmat[n - 1] = (tri_r + (n - 1) * rows == pos[...]).astype(F32).astype(BF16)
+            g = n - 1
+            line = lax.broadcasted_iota(I32, (64, rows), 0)
+            for j, (k, q, core) in enumerate(BLOCKS[g]):
+                first = ((g * 8 + q) * 2 + core) * 64
+                pmat[g, pl.ds(j * 64, 64), :] = (line + first == pos[k]).astype(F32).astype(BF16)
         else:
-            line = jnp.where(tri_r == tri_c, pos[...], 0)
+            line = jnp.where(tri_r == tri_c, pos[0], 0)
             column = jnp.sum(line.astype(F32), axis=1, keepdims=True).astype(I32)
             umat[n - 3] = (tri_c + (n - 3) * rows == column).astype(F32).astype(BF16)
 
-    for name in ("own", "keep1", "sib1", "keep2", "sib2"):
+    for name in ("keep1", "sib1", "keep2", "sib2"):
         loads[name].wait()
 
     def level2(i):
         arrived(side.at[part(i)], side_s.at[i], side_r.at[i], side_dev)
         level(2, cur2, side, cur3, i)
-
-    def relay(col):
-        @pl.when(step < 3)
-        def _():
-            for p in range(PIECES):
-                chain_arrived(col * PIECES + p)
-                chain(col * PIECES + p).start()
+        for n, slot in enumerate((0, 2, 1)):
+            send(cur3.at[part(i)], wide.at[slot, part(i)], cast_s.at[n, i], cast_r.at[slot, i], beside[n + 1])
+        level(2, side, cur2, cur3x, i)
+
+    def hand_on(pieces):
+        for n in pieces:
+            chain_arrived(n)
+            chain(n).start()
+
+    def relay(point):
+        for place, pieces in enumerate(RELAY[point]):
+            if pieces:
+                pl.when(step == place)(lambda pieces=pieces: hand_on(pieces))
 
     for i in range(CHUNKS):
         arrived(far.at[part(i)], far_s.at[i], far_r.at[i], far_dev)
@@ -195,92 +231,125 @@
         if i < 5:
             prepare(i)
     level2(CHUNKS - 1)
+    relay(0)
 
     def block(ref, g, q, core):
         return ref.at[pl.ds(((g * 8 + q) * 2 + core) * 64, 64)]
 
+    def reach(q, s):
+        dx, dy = REACH[q][s]
+        return at(dx * hot, dy, s)
+
     def source(q, s):
-        dx, dy = REACH[q][0]
-        ex, ey = REACH[q][1]
-        return at(jnp.where(c == 0, -dx, -ex), jnp.where(c == 0, -dy, -ey), s)
+        (dx, dy), (ex, ey) = REACH[q]
+        return at(jnp.where(c == 0, dx, ex) * hot, jnp.where(c == 0, -dy, -ey), s)
 
     def number(g, q, s):
         return (g * 8 + q) * 2 + s
 
-    def rows_send(g, q):
-        if q == 0:
-            send(block(packed, g, 0, 1 - c), rbuf.at[g, 0, 0], d_s.at[g * 16], d_r.at[g * 16], twin_dev)
+    forward = {
+        (1, 2, 0): at(0, 1, 0), (1, 3, 0): at(0, -1, 0), (1, 1, 0): at(-hot, 0, 0),
+        (2, 2, 1): at(0, -1, 1), (2, 3, 1): at(0, 1, 1), (3, 1, 1): at(0, 1, 1), (4, 1, 1): at(0, -1, 1),
+    }
+
+    def pack(g, k):
+        places = [j for j, entry in enumerate(BLOCKS[g]) if entry[0] == k]
+        rows_of = cur3 if k == 0 else cur3x if k == 1 else wide.at[k - 2]
+        span = pl.ds(places[0] * 64, len(places) * 64)
+        base = g * 1024
+        packed[pl.ds(base + places[0] * 64, len(places) * 64)] = jnp.dot(
+            pmat[g, span, :], rows_of[...], preferred_element_type=F32).astype(BF16)
+        for j in places:
+            entry = BLOCKS[g][j]
+            n = number(g, entry[1], c)
+            if entry in forward:
+                send(packed.at[pl.ds(base + j * 64, 64)], rbuf.at[g, entry[1], c],
+                     d_s.at[g * 16 + j], d_r.at[n], forward[entry])
+            elif entry[2] == 0:
+                q = entry[1]
+                send(packed.at[pl.ds(base + (j + 1 - c) * 64, 64)], rbuf.at[g, q, c],
+                     d_s.at[g * 16 + j], d_r.at[n], twin_dev)
+                rbuf[g, q, c] = packed[pl.ds(base + (j + c) * 64, 64)]
+
+    def rows_arrived(g, q):
+        if q in (1, 2, 3):
+            for s in range(2):
+                n = number(g, q, s)
+                arrived(rbuf.at[g, q, s], d_s.at[n], d_r.at[n], twin_dev)
             return
+        n = number(g, q, 1 - c)
+        arrived(rbuf.at[g, q, 1 - c], d_s.at[n], d_r.at[n], twin_dev)
+
+    def couple(g, e):
+        lines = pl.ds(e * 32, 32)
+        left = rbuf[g, :, :, lines, :].reshape(512, modes)
+        product = jnp.dot(left, wall[g * 2 + e], preferred_element_type=F32)
+        res[g, :, :, lines, :] = product.astype(BF16).reshape(8, 2, 32, modes)
+
+    def share(g, e):
+        return pl.ds(e * 32, 32 if g else 64)
+
+    def result_send(g, q, e=0):
+        part_of = share(g, e)
         for s in range(2):
-            send(block(packed, g, q, s), rbuf.at[g, q, c],
-                 d_s.at[number(g, q, s)], d_r.at[number(g, q, c)], at(*REACH[q][s], s))
-
-    def pack(g, k):
-        packed[pl.ds(g * 1024 + k * 256, 256)] = jnp.dot(
-            pmat[g, pl.ds(k * 256, 256), :], cur3[...], preferred_element_type=F32).astype(BF16)
-        if k == 0:
-            rbuf[g, 0, 1] = packed[pl.ds(g * 1024 + c * 64, 64)]
-
-    def rows_arrived(g, q):
-        if q == 0:
-            arrived(rbuf.at[g, 0, 0], d_s.at[g * 16], d_r.at[g * 16], twin_dev)
-            return
-        for s in range(2):
-            n = number(g, q, s)
-            arrived(rbuf.at[g, q, s], d_s.at[n], d_r.at[n], source(q, s))
-
-    def couple(g):
-        for e in range(2):
-            lines = pl.ds(e * 32, 32)
-            left = rbuf[g, :, :, lines, :].reshape(512, modes)
-            product = jnp.dot(left, wall[g * 2 + e], preferred_element_type=F32)
-            res[g, :, :, lines, :] = product.astype(BF16).reshape(8, 2, 32, modes)
-
-    def result_send(g, q):
-        if q == 0:
-            send(res.at[g, 0, 0], block(ret, g, 0, c), b_s.at[g * 16], b_r.at[g * 16], twin_dev)
-            ret[pl.ds(g * 1024 + c * 64, 64)] = res[g, 0, 1]
-            return
-        for s in range(2):
-            send(res.at[g, q, s], block(ret, g, q, c), b_s.at[number(g, q, s)], b_r.at[number(g, q, c)], source(q, s))
-
-    def result_arrived(g, q):
-        if q == 0:
-            arrived(block(ret, g, 0, 1 - c), b_s.at[g * 16], b_r.at[g * 16], twin_dev)
-            return
-        for s in range(2):
-            n = number(g, q, s)
-            arrived(block(ret, g, q, s), b_s.at[n], b_r.at[n], at(*REACH[q][s], s))
-
-    for g in range(2):
-        for k in range(4):
+            if q == 0 and s == 1:
+                first = g * 1024 + c * 64 + e * 32
+                ret[pl.ds(first, part_of.size)] = res[g, 0, c, part_of]
+                continue
+            core = 1 - c if q == 0 else s
+            sent, got = number(g + e, q, s), number(g + e, q, 0 if q == 0 else c)
+            send(res.at[g, q, core, part_of], block(ret, g, q, c).at[part_of], b_s.at[sent], b_r.at[got],
+                 twin_dev if q == 0 else source(q, s))
+
+    def result_arrived(g, q, e=0):
+        part_of = share(g, e)
+        for s in range(1 if q == 0 else 2):
+            n = number(g + e, q, s)
+            core, dev = (1 - c, twin_dev) if q == 0 else (s, reach(q, s))
+            arrived(block(ret, g, q, core).at[part_of], b_s.at[n], b_r.at[n], dev)
+
+    for k in (1, 0):
+        for g in range(2):
             pack(g, k)
-            for q in (2 * k + 1, 2 * k):
-                rows_send(g, q)
-        relay(g)
+    relay(1)
+    for k in (2, 3, 4):
+        for i in range(CHUNKS):
+            arrived(wide.at[k - 2, part(i)], cast_s.at[0, i], cast_r.at[k - 2, i], beside[k - 1])
+        for g in range(2):
+            pack(g, k)
+        if k == 2:
+            relay(2)
+    relay(3)
     for q in range(8):
         rows_arrived(0, q)
-    couple(0)
-    for q in (1, 2, 3, 4, 5, 6, 7, 0):
+    order = (1, 2, 3, 4, 5, 6, 7, 0)
+    couple(0, 0)
+    couple(0, 1)
+    for q in order:
         result_send(0, q)
-
-    @pl.when(step == 3)
-    def _():
-        for n in range(2 * PIECES):
-            chain_arrived(n)
+    relay(4)
     for q in range(8):
         rows_arrived(1, q)
-    couple(1)
-    for q in (1, 2, 3, 4, 5, 6, 7, 0):
-        result_send(1, q)
+    for e in range(2):
+        @pl.when(step == 3)
+        def _():
+            for n in range(e * PIECES, (e + 1) * PIECES):
+                chain_arrived(n)
+        couple(1, e)
+        for q in order:
+            result_send(1, q, e)
+        if e == 0:
+            relay(5)
     for q in range(8):
         result_arrived(0, q)
     acc[...] = jnp.dot(umat[0], ret[pl.ds(0, 1024)], preferred_element_type=F32)
     for q in range(4, 8):
-        result_arrived(1, q)
+        result_arrived(1, q, 0)
+        result_arrived(1, q, 1)
     acc[...] += jnp.dot(umat[1, :, 512:], ret[pl.ds(1536, 512)], preferred_element_type=F32)
     for q in range(4):
-        result_arrived(1, q)
+        result_arrived(1, q, 0)
+        result_arrived(1, q, 1)
     got = jnp.dot(umat[1, :, :512], ret[pl.ds(1024, 512)], preferred_element_type=F32)
     out_ref[...] = (acc[...] + got).astype(BF16)
 
@@ -301,12 +370,14 @@
         out_specs=vmem,
         scratch_shapes=[
             pltpu.VMEM((rows, modes), BF16),
-            pltpu.VMEM((1, rows), I32),
+            pltpu.VMEM((5, 1, rows), I32),
             pltpu.VMEM(keep_proj.shape, BF16),
             pltpu.VMEM(sibling_proj.shape, BF16),
             pltpu.VMEM(coupling.shape, BF16),
             pltpu.VMEM(pattern.shape, I32),
             dma((10,)),
+            pltpu.VMEM((rows, modes), BF16),
+            pltpu.VMEM((3, rows, modes), BF16),
         ]
         + [pltpu.VMEM((rows, modes), BF16)] * 6
         + [
@@ -318,12 +389,17 @@
             pltpu.VMEM((2, rows, rows), BF16),
             pltpu.VMEM((2, rows, rows), BF16),
             pltpu.VMEM((rows, modes), F32),
-            pltpu.VMEM((1, rows), I32),
+            pltpu.VMEM((5, 1, rows), I32),
+            dma((4,)),
+            dma((4,)),
+            dma((3, CHUNKS)),
+            dma((3, CHUNKS)),
         ]
         + [dma((CHUNKS,))] * 6
         + [dma((2 * PIECES,))] * 2
         + [dma((1,))] * 2
-        + [dma((32,))] * 4,
+        + [dma((32,))] * 2
+        + [dma((48,))] * 2,
         compiler_params=pltpu.CompilerParams(
             collective_id=0, has_side_effects=True, vmem_limit_bytes=56 << 20),
         name="condense",

time: 102 us -> 99.4 us (0.975)
  Pallas kernels: 100 us -> 97 us
    pallas_call x1, Pallas kernels: 100 us -> 97 us  [local(): pl.pallas_call(kernel, out_shape=pltpu.VMEM((rows, modes), BF16), in_spec...]
where the time goes in v4:
time: 99.4 us; the launch traced here: 98 us
  Pallas kernels  97 us (98%)
    pallas_call x1, Pallas kernels, local(): pl.pallas_call(kernel, out_shape=pltpu.VMEM((rows, modes), BF16), in_spec...  97 us

profile of v4, /device:TPU:33, one launch (start us, length us, event | category | flops | bytes accessed | tf_op | source)
XLA Modules:
  0.0 98.0 jit_solution(17092518064952329466)
XLA Ops:
  0.0 97.0 %condense.1 = bf16[1024,512]{1,0:T(8,128)(2,1)S(1)} custom-call(bf16[1024,512]{1,0:T(8,128)(2,1)} %x_hbm.1, s32[1,1024]{1,0:T(1,128)} %bitcast.1, bf16[3,512,512]{2,1,0:T(8,128)(2,1)} %keep_hbm.1, bf16[3,512,512]{2,1,0:T(8,128)(2,1)} %sib_hbm.1, bf16[1,512,512]{2,1,0:T(8,128)(2,1)} %coup_hbm.1, s32[1,8,8]{2,1,0:T(8,128)} %pat_hbm.1), custom_call_target="tpu_custom_call" | custom-call | tf_op jit(solution)/shard_map/condense/pallas_call | solution.py:366
  97.0 1.0 copy.8

commit v5 on v4

--- a/solution.py
+++ b/solution.py
@@ -122,14 +122,16 @@
     def far_send(i):
         send(cur1.at[part(i)], far.at[part(i)], far_s.at[i], far_r.at[i], far_dev)
 
-    for name in ("x", "keep0", "sib0", "own"):
+    for name in ("x", "keep0", "sib0"):
         loads[name].wait()
-    for n, slot in enumerate((1, 2, 4, 3)):
-        send(own_all.at[0], own_all.at[slot], own_s.at[n], own_r.at[slot - 1], beside[n])
     for i in range(CHUNKS):
         arrived(twin.at[part(i)], twin_s.at[i], twin_r.at[i], twin_dev)
         level(0, x_ref, twin, cur1, i)
         far_send(i)
+
+    loads["own"].wait()
+    for n, slot in enumerate((1, 2, 4, 3)):
+        send(own_all.at[0], own_all.at[slot], own_s.at[n], own_r.at[slot - 1], beside[n])
 
     loads["coup"].wait()
     loads["pat"].wait()
@@ -217,7 +219,7 @@
 
     for i in range(CHUNKS):
         arrived(far.at[part(i)], far_s.at[i], far_r.at[i], far_dev)
-        if i == CHUNKS - 1:
+        if i == CHUNKS - 2:
             arrived(wall.at[1 - upper], g_s.at[0], g_r.at[0], pair_dev)
 
             @pl.when(step == 3)

time: 99.4 us -> 99.2 us (level)
  no operation moved by 1% of the time
where the time goes in v5:
time: 99.2 us; the launch traced here: 97.7 us
  Pallas kernels  96.8 us (98%)
    pallas_call x1, Pallas kernels, local(): pl.pallas_call(kernel, out_shape=pltpu.VMEM((rows, modes), BF16), in_spec...  96.8 us

profile of v5, /device:TPU:33, one launch (start us, length us, event | category | flops | bytes accessed | tf_op | source)
XLA Modules:
  0.0 97.7 jit_solution(16428959627585328896)
XLA Ops:
  0.0 96.8 %condense.1 = bf16[1024,512]{1,0:T(8,128)(2,1)S(1)} custom-call(bf16[1024,512]{1,0:T(8,128)(2,1)} %x_hbm.1, s32[1,1024]{1,0:T(1,128)} %bitcast.1, bf16[3,512,512]{2,1,0:T(8,128)(2,1)} %keep_hbm.1, bf16[3,512,512]{2,1,0:T(8,128)(2,1)} %sib_hbm.1, bf16[1,512,512]{2,1,0:T(8,128)(2,1)} %coup_hbm.1, s32[1,8,8]{2,1,0:T(8,128)} %pat_hbm.1), custom_call_target="tpu_custom_call" | custom-call | tf_op jit(solution)/shard_map/condense/pallas_call | solution.py:368
  96.8 1.0 copy.8

commit v6 on v5

--- a/solution.py
+++ b/solution.py
@@ -8,7 +8,7 @@
 BS = 64
 LEVELS = 3
 EPS = 1e-06
-SIZES = (128, 128, 128, 128, 128, 128, 128, 64, 64)
+SIZES = (64, 128, 128, 128, 128, 128, 128, 128, 64)
 CHUNKS = len(SIZES)
 PIECES = 4
 RELAY = (

time: 99.2 us -> 97.9 us (0.987)
  no operation moved by 1% of the time
where the time goes in v6:
time: 97.9 us; the launch traced here: 97.1 us
  Pallas kernels  96.1 us (98%)
    pallas_call x1, Pallas kernels, local(): pl.pallas_call(kernel, out_shape=pltpu.VMEM((rows, modes), BF16), in_spec...  96.1 us

profile of v6, /device:TPU:33, one launch (start us, length us, event | category | flops | bytes accessed | tf_op | source)
XLA Modules:
  0.0 97.1 jit_solution(17284515236456942809)
XLA Ops:
  0.0 96.1 %condense.1 = bf16[1024,512]{1,0:T(8,128)(2,1)S(1)} custom-call(bf16[1024,512]{1,0:T(8,128)(2,1)} %x_hbm.1, s32[1,1024]{1,0:T(1,128)} %bitcast.1, bf16[3,512,512]{2,1,0:T(8,128)(2,1)} %keep_hbm.1, bf16[3,512,512]{2,1,0:T(8,128)(2,1)} %sib_hbm.1, bf16[1,512,512]{2,1,0:T(8,128)(2,1)} %coup_hbm.1, s32[1,8,8]{2,1,0:T(8,128)} %pat_hbm.1), custom_call_target="tpu_custom_call" | custom-call | tf_op jit(solution)/shard_map/condense/pallas_call | solution.py:368
  96.1 1.0 %copy.8 = bf16[1024,512]{1,0:T(8,128)(2,1)} copy(bf16[1024,512]{1,0:T(8,128)(2,1)S(1)} %condense.1) | data formatting | bytes 2097152
